TPU v7x, 256 devices: a whole 4x4x8 slice. The times are simulated.
256 devices in a mesh: row: 32 (over x, y, core), col: 8 (over z).
Axes of the slice: x: 4, y: 4, z: 8, core: 2. Of those that a mesh axis runs over, the one named last changes fastest.
Arguments:
- kernel_tiles: float32 [32, 8, 9, 256, 512], P('row', 'col'), may hold values from -0.09375 to 0.09375
- footprints: int32 [32, 8, 9], P('row', 'col'), may hold values from 0 to 8, as said below
- counts: int32 [32, 8], P('row', 'col'), may hold values from 64 to 256, as said below
- readings: float32 [32, 8, 256], P('row', 'col'), may hold values from -6 to 6
- damping: float32 [1], replicated, may hold values from 0.1 to 0.5
- layer_depth: float32 [2], replicated, may hold values from 1 to 6
- inclinations: float32 [2], replicated, may hold values from 0.6 to 1.3
- declinations: float32 [2], replicated, may hold values from -3.140625 to 3.140625
- resid_grid: float32 [4096, 4096], P('col', 'row'), may hold values from -3 to 3
Outputs:
- coefficients: float32 [32, 8, 512], P('row', 'col')
- rtp_map: float32 [4096, 4096], P(('row', 'col'))
Inputs may be any that keep to these rules, and one draw needn't show every extreme that they name: `footprints`: each tile's list holds each of the 9 codes once; code 3 (a + 1) + (b + 1) names the source block a tiles north and b tiles east of the tile; blocks outside the survey are empty. `counts`: reading slots from this count on are ignored.
All inputs are finite; a program needn't handle non-finite values.
Results may differ from a plain program's by a relative error of at most 0.0003.
Values sent between devices are 32-bit elements; how exact they have to be, the bound alone decides.
A program may use at most 128 MiB of HBM per device.

v0:
```python
import math
import jax
import jax.numpy as jnp
from jax import lax
from jax.sharding import PartitionSpec as P

SRC_ROWS = 8
SRC_COLS = 32
LAYERS = 2
REFINE = 16
INNER_LEN = 128
FOOTPRINT = 9
CG_STEPS = 2
HIGHEST_PRECISION = lax.Precision.HIGHEST
NEIGHBOUR_OFFSETS = tuple(
    ((north_step, east_step) for north_step in (-1, 0, 1) for east_step in (-1, 0, 1))
)


def shifted(x, axis, by):
    peers = lax.axis_size(axis)
    pairs = [(i, i + by) for i in range(peers) if 0 <= i + by < peers]
    return lax.ppermute(x, axis, pairs)


def hat_table(fine_start, fine_count, coarse_start, coarse_count):
    fine_pos = jnp.arange(fine_count, dtype=jnp.float32) + fine_start
    coarse_pos = jnp.arange(coarse_count, dtype=jnp.float32) + coarse_start
    offset = (fine_pos[:, None] + 0.5) / REFINE - 0.5 - coarse_pos[None, :]
    return jnp.maximum(0.0, 1.0 - jnp.abs(offset))


def frequency_of(positions, full_len):
    signed = jnp.where(positions < full_len // 2, positions, positions - full_len)
    return signed.astype(jnp.float32) / full_len


def pole_filter(north_freq, east_freq, inclinations, declinations):
    radius = jnp.sqrt(north_freq * north_freq + east_freq * east_freq)
    safe_radius = jnp.where(radius > 0.0, radius, 1.0)
    unit_north = jnp.where(radius > 0.0, north_freq / safe_radius, 0.0)
    unit_east = jnp.where(radius > 0.0, east_freq / safe_radius, 0.0)
    real_part = jnp.ones_like(radius)
    imag_part = jnp.zeros_like(radius)
    for member in range(2):
        vertical = jnp.sin(inclinations[member])
        horizontal = jnp.cos(inclinations[member])
        along_axis = horizontal * (
            jnp.cos(declinations[member]) * unit_north + jnp.sin(declinations[member]) * unit_east
        )
        denominator = vertical * vertical + along_axis * along_axis
        inv_real = vertical / denominator
        inv_imag = -along_axis / denominator
        real_part, imag_part = (
            real_part * inv_real - imag_part * inv_imag,
            real_part * inv_imag + imag_part * inv_real,
        )
    return (real_part, imag_part)


def phase_table(row_len, col_len, period, direction_sign):
    product = (
        jnp.arange(row_len, dtype=jnp.int32)[:, None]
        * jnp.arange(col_len, dtype=jnp.int32)[None, :]
        % period
    )
    angle = 2.0 * math.pi / period * product.astype(jnp.float32)
    return (jnp.cos(angle), direction_sign * jnp.sin(angle))


def transform_last(real_in, imag_in, direction_sign):
    dims_in = real_in.shape
    length = dims_in[-1]
    outer_len = length // INNER_LEN
    real_blocks = real_in.reshape(-1, outer_len, INNER_LEN)
    cos_outer, sin_outer = phase_table(outer_len, outer_len, outer_len, direction_sign)
    first_real = jnp.einsum("man,ak->mkn", real_blocks, cos_outer, precision=HIGHEST_PRECISION)
    first_imag = jnp.einsum("man,ak->mkn", real_blocks, sin_outer, precision=HIGHEST_PRECISION)
    if imag_in is not None:
        imag_blocks = imag_in.reshape(-1, outer_len, INNER_LEN)
        first_real = first_real - jnp.einsum(
            "man,ak->mkn", imag_blocks, sin_outer, precision=HIGHEST_PRECISION
        )
        first_imag = first_imag + jnp.einsum(
            "man,ak->mkn", imag_blocks, cos_outer, precision=HIGHEST_PRECISION
        )
    twist_cos, twist_sin = phase_table(outer_len, INNER_LEN, length, direction_sign)
    turned_real = first_real * twist_cos - first_imag * twist_sin
    turned_imag = first_real * twist_sin + first_imag * twist_cos
    cos_inner, sin_inner = phase_table(INNER_LEN, INNER_LEN, INNER_LEN, direction_sign)
    final_real = jnp.einsum(
        "mkn,nj->mjk", turned_real, cos_inner, precision=HIGHEST_PRECISION
    ) - jnp.einsum("mkn,nj->mjk", turned_imag, sin_inner, precision=HIGHEST_PRECISION)
    final_imag = jnp.einsum(
        "mkn,nj->mjk", turned_real, sin_inner, precision=HIGHEST_PRECISION
    ) + jnp.einsum("mkn,nj->mjk", turned_imag, cos_inner, precision=HIGHEST_PRECISION)
    return (final_real.reshape(dims_in), final_imag.reshape(dims_in))


def neighbour_block(values, step_by, keep_mask):
    arrived = shifted(values, ("row", "col"), step_by)
    return jnp.where(keep_mask, arrived, 0.0)


def collect_blocks(own_block, col_count, col_index):
    pieces = []
    for north_step, east_step in NEIGHBOUR_OFFSETS:
        if north_step == 0 and east_step == 0:
            pieces.append(own_block)
        else:
            source_col = col_index + east_step
            keep_mask = (source_col >= 0) & (source_col < col_count)
            pieces.append(
                neighbour_block(own_block, -(north_step * col_count + east_step), keep_mask)
            )
    return jnp.stack(pieces)


def return_blocks(spread, col_count, col_index):
    summed = spread[4]
    for position, (north_step, east_step) in enumerate(NEIGHBOUR_OFFSETS):
        if north_step != 0 or east_step != 0:
            source_col = col_index - east_step
            keep_mask = (source_col >= 0) & (source_col < col_count)
            summed = summed + neighbour_block(
                spread[position], north_step * col_count + east_step, keep_mask
            )
    return summed


def local_coarse(solution, col_count, col_index):
    final_blocks = collect_blocks(solution, col_count, col_index)
    coarse = final_blocks.reshape(3, 3, LAYERS, SRC_ROWS, SRC_COLS).transpose(2, 0, 3, 1, 4)
    return coarse.reshape(LAYERS, 3 * SRC_ROWS, 3 * SRC_COLS)


def squares(residual):
    return lax.psum(jnp.sum(residual * residual), ("row", "col"))


def on_device(
    kernel_tiles,
    footprints,
    counts,
    readings,
    damping,
    layer_depth,
    inclinations,
    declinations,
    resid_grid,
):
    col_count = lax.axis_size("col")
    row_count = lax.axis_size("row")
    col_index = lax.axis_index("col")
    row_index = lax.axis_index("row")
    kernels = kernel_tiles[0, 0]
    selector = (
        footprints[0, 0][:, None] == jnp.arange(FOOTPRINT, dtype=jnp.int32)[None, :]
    ).astype(jnp.float32)
    live_mask = (jnp.arange(kernels.shape[1], dtype=jnp.int32) < counts[0, 0]).astype(jnp.float32)
    ridge_weight = damping[0]

    def adjoint(values):
        partial_sums = jnp.einsum(
            "krs,r->ks", kernels, live_mask * values, precision=HIGHEST_PRECISION
        )
        spread = jnp.dot(selector.T, partial_sums, precision=HIGHEST_PRECISION)
        return return_blocks(spread, col_count, col_index)

    right_side = adjoint(readings[0, 0])
    solution = jnp.zeros_like(right_side)
    residual = right_side
    direction = right_side
    norm_now = squares(residual)
    for iteration in range(CG_STEPS):
        blocks = collect_blocks(direction, col_count, col_index)
        chosen = jnp.dot(selector, blocks, precision=HIGHEST_PRECISION)
        applied = (
            adjoint(
                live_mask * jnp.einsum("krs,ks->r", kernels, chosen, precision=HIGHEST_PRECISION)
            )
            + ridge_weight * direction
        )
        step_size = norm_now / lax.psum(jnp.sum(direction * applied), ("row", "col"))
        solution = solution + step_size * direction
        residual = residual - step_size * applied
        if iteration + 1 < CG_STEPS:
            norm_next = squares(residual)
            direction = residual + norm_next / norm_now * direction
            norm_now = norm_next
    tile_east, tile_north = resid_grid.shape
    slab_rows = tile_north // col_count
    coarse = local_coarse(solution, col_count, col_index)
    up_north = hat_table(0.0, tile_north, -float(SRC_ROWS), 3 * SRC_ROWS)
    up_east = hat_table(0.0, tile_east, -float(SRC_COLS), 3 * SRC_COLS)
    eastward = jnp.einsum("lgh,vh->lgv", coarse, up_east, precision=HIGHEST_PRECISION)
    model_planes = jnp.einsum("lgv,ug->lvu", eastward, up_north, precision=HIGHEST_PRECISION)
    tile_planes = jnp.concatenate([model_planes, resid_grid[None]], axis=0)
    planes = lax.all_to_all(tile_planes, "row", split_axis=1, concat_axis=2, tiled=True)
    full_north = planes.shape[-1]
    north_real, north_imag = transform_last(planes, None, -1.0)
    spectra = jnp.stack([north_real, north_imag])
    slab = lax.all_to_all(
        lax.all_to_all(spectra, "row", split_axis=3, concat_axis=2, tiled=True),
        "col",
        split_axis=3,
        concat_axis=2,
        tiled=True,
    )
    slab = jnp.swapaxes(slab, 2, 3)
    full_east = slab.shape[3]
    east_real, east_imag = transform_last(slab[0], slab[1], -1.0)
    north_index = (
        row_index * tile_north + col_index * slab_rows + jnp.arange(slab_rows, dtype=jnp.int32)
    )
    north_freq = frequency_of(north_index, full_north)[:, None]
    east_freq = frequency_of(jnp.arange(full_east, dtype=jnp.int32), full_east)[None, :]
    wavenumber = 2.0 * math.pi * jnp.sqrt(north_freq * north_freq + east_freq * east_freq)
    combined_real = east_real[-1]
    combined_imag = east_imag[-1]
    for layer in range(LAYERS):
        layer_real, layer_imag = (east_real[layer], east_imag[layer])
        damped = jnp.exp(-wavenumber * layer_depth[layer])
        combined_real = combined_real + damped * layer_real
        combined_imag = combined_imag + damped * layer_imag
    filt_real, filt_imag = pole_filter(north_freq, east_freq, inclinations, declinations)
    shaped_real = filt_real * combined_real - filt_imag * combined_imag
    shaped_imag = filt_real * combined_imag + filt_imag * combined_real
    back_real, back_imag = transform_last(shaped_real, shaped_imag, 1.0)
    stacked = jnp.stack([back_real, back_imag]) / full_east
    returned = lax.all_to_all(
        lax.all_to_all(stacked, "row", split_axis=2, concat_axis=1, tiled=True),
        "col",
        split_axis=2,
        concat_axis=1,
        tiled=True,
    )
    returned = jnp.swapaxes(returned, 1, 2)
    out_cols = returned.shape[1]
    ordered = returned.reshape(2, out_cols, col_count, row_count, slab_rows).transpose(
        0, 1, 3, 2, 4
    )
    ordered = ordered.reshape(2, out_cols, full_north)
    final_real, final_imag = transform_last(ordered[0], ordered[1], 1.0)
    rtp_map = final_real / full_north
    return (solution.reshape(1, 1, -1), rtp_map)


def solution(mesh):
    in_specs = (
        P("row", "col", None, None, None),
        P("row", "col", None),
        P("row", "col"),
        P("row", "col", None),
        P(),
        P(),
        P(),
        P(),
        P("col", "row"),
    )
    out_specs = (P("row", "col", None), P(("row", "col"), None))
    return jax.shard_map(
        on_device, mesh=mesh, in_specs=in_specs, out_specs=out_specs, check_vma=False
    )
```

profile of v0, /device:TPU:1, one launch (start us, length us, event | category | flops | bytes accessed | tf_op | source)
XLA Modules:
  0.0 759.6 jit_solution(11323980032133279021)
XLA Ops:
  1.3 4.7 fusion.8
  7.6 5.1 collective-permute-start.1
  14.7 5.0 collective-permute-start.3
  21.6 7.7 %collective-permute-start.5 = (f32[512]{0:T(512)S(1)}, f32[512]{0:T(512)S(1)}, u32[]{:S(2)}, u32[]{:S(2)}) collective-permute-start(f32[512]{0:T(512)S(1)} %bitcast.347), channel_id=1, source_target_pairs={{0,7},{1,8},{2,9},{3,10},{4,11},{5,12},{6,13},{7,14},{8,15},{9,16}... | collective-permute-start | bytes 6152 | tf_op jit(solution)/shard_map/ppermute | solution.py:23
  29.4 5.0 collective-permute-start.6
  36.4 6.2 collective-permute-start.10
  42.6 5.2 collective-permute-start.11
  53.0 5.2 collective-permute-start.8
  58.2 3.9 collective-permute-start.9
  64.1 2.9 collective-permute-done.14
  67.3 6.2 fusion.6
  73.5 2.3 fusion.4
  81.3 4.4 collective-permute-start.19
  87.7 9.0 %collective-permute-start.21 = (f32[512]{0:T(512)S(1)}, f32[512]{0:T(512)S(1)}, u32[]{:S(2)}, u32[]{:S(2)}) collective-permute-start(f32[512]{0:T(512)S(1)} %bitcast.355), channel_id=1, source_target_pairs={{0,7},{1,8},{2,9},{3,10},{4,11},{5,12},{6,13},{7,14},{8,15},{9,16}... | collective-permute-start | bytes 6152 | tf_op jit(solution)/shard_map/ppermute | solution.py:23
  96.7 3.7 collective-permute-start.22
  100.4 2.8 collective-permute-start.23
  104.6 91.9 %all-reduce = (f32[]{:T(128)}, f32[]{:T(128)}) all-reduce(f32[]{:T(128)} %get-tuple-element.3, f32[]{:T(128)} %get-tuple-element.2), channel_id=1, replica_groups=mesh['row'=32,'col'=8] {'row','col'}, use_global_device_ids=true, to_apply=%region_1.2 | all-reduce | flops 2 | bytes 16 | tf_op jit(solution)/shard_map/psum | solution.py:138
  198.5 74.3 %psum.30 = f32[]{:T(128)} all-reduce(f32[]{:T(128)} %multiply_reduce_fusion.1), channel_id=1, replica_groups=mesh['row'=32,'col'=8] {'row','col'}, use_global_device_ids=true, to_apply=%region_5.6 | all-reduce | flops 1 | bytes 8 | tf_op jit(solution)/shard_map/psum | solution.py:138
  274.2 2.7 collective-permute-start.26
  276.9 3.9 collective-permute-start.27
  280.8 2.9 collective-permute-start.28
  287.1 5.4 collective-permute-start.25
  294.5 3.5 collective-permute-start.24
  298.9 6.1 fusion.2
  305.0 4.7 fusion
  315.2 4.7 collective-permute-start.35
  321.8 8.8 %collective-permute-start.37 = (f32[512]{0:T(512)S(1)}, f32[512]{0:T(512)S(1)}, u32[]{:S(2)}, u32[]{:S(2)}) collective-permute-start(f32[512]{0:T(512)S(1)} %bitcast.354), channel_id=1, source_target_pairs={{0,7},{1,8},{2,9},{3,10},{4,11},{5,12},{6,13},{7,14},{8,15},{9,16}... | collective-permute-start | bytes 6152 | tf_op jit(solution)/shard_map/ppermute | solution.py:23
  330.7 4.2 collective-permute-start.38
  334.8 3.4 collective-permute-start.39
  339.6 86.3 %psum.31 = f32[]{:T(128)} all-reduce(f32[]{:T(128)} %multiply_reduce_fusion), channel_id=1, replica_groups=mesh['row'=32,'col'=8] {'row','col'}, use_global_device_ids=true, to_apply=%region_7.8 | all-reduce | flops 1 | bytes 8 | tf_op jit(solution)/shard_map/psum | solution.py:184
  427.2 3.7 collective-permute-start.42
  430.9 2.2 collective-permute-start.43
  433.1 4.6 collective-permute-start.44
  441.0 4.6 collective-permute-start.41
  447.5 4.2 collective-permute-start.40
  455.8 16.3 %all-to-all-start = ((f32[3,512,128]{2,0,1:T(4,128)}), f32[3,512,128]{2,0,1:T(4,128)S(1)}, u32[]{:S(2)}, u32[]{:S(2)}) async-start(f32[3,512,128]{2,0,1:T(4,128)} %copy.161), calls=%async_computation | async-start | bytes 2097152 | tf_op jit(solution)/shard_map/all_to_all | solution.py:199
  472.2 16.7 %all-to-all-done = f32[3,512,128]{2,0,1:T(4,128)S(1)} async-done(((f32[3,512,128]{2,0,1:T(4,128)}), f32[3,512,128]{2,0,1:T(4,128)S(1)}, u32[]{:S(2)}, u32[]{:S(2)}) %all-to-all-start) | async-done | bytes 786464 | tf_op jit(solution)/shard_map/all_to_all | solution.py:199
  492.7 2.4 fusion.26
  495.1 2.4 fusion.13
  497.4 2.0 copy.165
  499.4 2.3 stack_reshape.12
  501.8 3.7 fusion.12
  505.4 2.4 copy.168
  507.8 2.3 stack_reshape.13
  511.6 12.5 %copy.169 = f32[2,3,16,4096]{2,0,1,3:T(2,128)} copy(f32[2,3,16,4096]{3,2,1,0:T(8,128)S(1)} %pad_maximum_fusion) | data formatting | bytes 3145728 | tf_op jit(solution)/shard_map/stack | solution.py:202
  524.2 19.0 %reshape.239 = f32[32,1,12288]{2,1,0:T(1,128)S(1)} reshape(f32[4096,3,2,16]{3,2,1,0:T(2,128)} %bitcast.279) | data formatting | bytes 3145728
  543.2 26.6 %all_to_all.87 = f32[32,1,12288]{2,1,0:T(1,128)S(1)} all-to-all(f32[32,1,12288]{2,1,0:T(1,128)S(1)} %reshape.239), channel_id=1, replica_groups=mesh['row'=32,'col'=8] {'row'}, dimensions={0} | all-to-all | bytes 3145728 | tf_op jit(solution)/shard_map/all_to_all | solution.py:204
  570.3 4.4 reduce
  574.7 18.7 %reshape.240 = f32[4096,3,2,16]{3,2,1,0:T(2,128)} reshape(f32[32,12288]{1,0:T(8,128)S(1)} %reduce) | data formatting | bytes 3145728
  593.3 14.3 %copy.210 = f32[2,3,16,32,128]{4,2,3,1,0:T(8,128)S(1)} copy(f32[2,3,16,32,128]{2,0,1,4,3:T(2,128)} %bitcast.280) | data formatting | bytes 3145728 | tf_op jit(solution)/shard_map/all_to_all | solution.py:204
  607.7 2.1 copy.172
  609.9 3.8 all-to-all-start.2
  621.2 32.7 %all-to-all-done.2 = f32[2,3,512,128]{2,0,1,3:T(2,128)S(1)} async-done(((f32[2,3,512,128]{2,0,1,3:T(2,128)}), f32[2,3,512,128]{2,0,1,3:T(2,128)S(1)}, u32[]{:S(2)}, u32[]{:S(2)}) %all-to-all-start.2) | async-done | bytes 1572896 | tf_op jit(solution)/shard_map/all_to_all | solution.py:203
  677.9 4.4 copy.187
  682.3 7.6 reshape.241
  689.8 15.2 %all_to_all.88 = f32[32,1,4096]{2,1,0:T(1,128)S(1)} all-to-all(f32[32,1,4096]{2,1,0:T(1,128)S(1)} %reshape.241), channel_id=1, replica_groups=mesh['row'=32,'col'=8] {'row'}, dimensions={0} | all-to-all | bytes 1048576 | tf_op jit(solution)/shard_map/all_to_all | solution.py:232
  706.9 7.0 reshape.242
  713.8 5.1 copy.212
  719.2 20.9 %all_to_all.89 = f32[2,512,128]{1,0,2:T(2,128)S(1)} all-to-all(f32[2,512,128]{1,0,2:T(2,128)S(1)} %copy.190), channel_id=1, replica_groups=mesh['row'=32,'col'=8] {'col'}, dimensions={2} | all-to-all | bytes 1048576 | tf_op jit(solution)/shard_map/all_to_all | solution.py:231
  740.2 2.8 reshape.220
  743.0 4.2 fusion.326
  747.3 2.2 copy.193
  749.5 1.9 fusion.138
  753.2 2.2 convolution_subtract_fusion.6
  (204 shorter events, 87.0 us)
Async XLA Ops:
  0.6 5.3 copy-start.3
  6.3 15.3 %collective-permute-start = (f32[512]{0:T(512)S(1)}, f32[512]{0:T(512)S(1)}, u32[]{:S(2)}, u32[]{:S(2)}) collective-permute-start(f32[512]{0:T(512)S(1)} %bitcast.367), channel_id=1, source_target_pairs={{9,0},{10,1},{11,2},{12,3},{13,4},{14,5},{15,6},{16,7},{17,8},{18,... | collective-permute-start | bytes 6152 | tf_op jit(solution)/shard_map/ppermute | solution.py:23
  7.6 21.8 %collective-permute-start.1 = (f32[512]{0:T(512)S(1)}, f32[512]{0:T(512)S(1)}, u32[]{:S(2)}, u32[]{:S(2)}) collective-permute-start(f32[512]{0:T(512)S(1)} %bitcast.364), channel_id=1, source_target_pairs={{8,0},{9,1},{10,2},{11,3},{12,4},{13,5},{14,6},{15,7},{16,8},{17,9... | collective-permute-start | bytes 6152 | tf_op jit(solution)/shard_map/ppermute | solution.py:23
  12.7 21.6 %collective-permute-start.2 = (f32[512]{0:T(512)S(1)}, f32[512]{0:T(512)S(1)}, u32[]{:S(2)}, u32[]{:S(2)}) collective-permute-start(f32[512]{0:T(512)S(1)} %bitcast.361), channel_id=1, source_target_pairs={{7,0},{8,1},{9,2},{10,3},{11,4},{12,5},{13,6},{14,7},{15,8},{16,9}... | collective-permute-start | bytes 6152 | tf_op jit(solution)/shard_map/ppermute | solution.py:23
  14.7 21.0 %collective-permute-start.3 = (f32[512]{0:T(512)S(1)}, f32[512]{0:T(512)S(1)}, u32[]{:S(2)}, u32[]{:S(2)}) collective-permute-start(f32[512]{0:T(512)S(1)} %bitcast.349), channel_id=1, source_target_pairs={{1,0},{2,1},{3,2},{4,3},{5,4},{6,5},{7,6},{8,7},{9,8},{10,9},{11,1... | collective-permute-start | bytes 6152 | tf_op jit(solution)/shard_map/ppermute | solution.py:23
  19.7 16.0 %collective-permute-start.4 = (f32[512]{0:T(512)S(1)}, f32[512]{0:T(512)S(1)}, u32[]{:S(2)}, u32[]{:S(2)}) collective-permute-start(f32[512]{0:T(512)S(1)} %bitcast.348), channel_id=1, source_target_pairs={{0,1},{1,2},{2,3},{3,4},{4,5},{5,6},{6,7},{7,8},{8,9},{9,10},{10,1... | collective-permute-start | bytes 6152 | tf_op jit(solution)/shard_map/ppermute | solution.py:23
  21.6 14.1 %collective-permute-start.5 = (f32[512]{0:T(512)S(1)}, f32[512]{0:T(512)S(1)}, u32[]{:S(2)}, u32[]{:S(2)}) collective-permute-start(f32[512]{0:T(512)S(1)} %bitcast.347), channel_id=1, source_target_pairs={{0,7},{1,8},{2,9},{3,10},{4,11},{5,12},{6,13},{7,14},{8,15},{9,16}... | collective-permute-start | bytes 6152 | tf_op jit(solution)/shard_map/ppermute | solution.py:23
  29.4 6.3 collective-permute-start.6
  34.3 2.0 collective-permute-start.7
  36.4 16.6 %collective-permute-start.10 = (f32[512]{0:T(512)S(1)}, f32[512]{0:T(512)S(1)}, u32[]{:S(2)}, u32[]{:S(2)}) collective-permute-start(f32[512]{0:T(512)S(1)} %select_add_fusion.1), channel_id=1, source_target_pairs={{0,7},{1,8},{2,9},{3,10},{4,11},{5,12},{6,13},{7,14},{8,15},{9,16}... | collective-permute-start | bytes 6152 | tf_op jit(solution)/shard_map/ppermute | solution.py:23
  42.6 15.6 %collective-permute-start.11 = (f32[512]{0:T(512)S(1)}, f32[512]{0:T(512)S(1)}, u32[]{:S(2)}, u32[]{:S(2)}) collective-permute-start(f32[512]{0:T(512)S(1)} %select_add_fusion.1), channel_id=1, source_target_pairs={{0,1},{1,2},{2,3},{3,4},{4,5},{5,6},{6,7},{7,8},{8,9},{9,10},{10,1... | collective-permute-start | bytes 6152 | tf_op jit(solution)/shard_map/ppermute | solution.py:23
  47.8 14.3 %collective-permute-start.12 = (f32[512]{0:T(512)S(1)}, f32[512]{0:T(512)S(1)}, u32[]{:S(2)}, u32[]{:S(2)}) collective-permute-start(f32[512]{0:T(512)S(1)} %select_add_fusion.1), channel_id=1, source_target_pairs={{1,0},{2,1},{3,2},{4,3},{5,4},{6,5},{7,6},{8,7},{9,8},{10,9},{11,1... | collective-permute-start | bytes 6152 | tf_op jit(solution)/shard_map/ppermute | solution.py:23
  49.7 14.3 %collective-permute-start.13 = (f32[512]{0:T(512)S(1)}, f32[512]{0:T(512)S(1)}, u32[]{:S(2)}, u32[]{:S(2)}) collective-permute-start(f32[512]{0:T(512)S(1)} %select_add_fusion.1), channel_id=1, source_target_pairs={{7,0},{8,1},{9,2},{10,3},{11,4},{12,5},{13,6},{14,7},{15,8},{16,9}... | collective-permute-start | bytes 6152 | tf_op jit(solution)/shard_map/ppermute | solution.py:23
  51.7 12.4 %collective-permute-start.15 = (f32[512]{0:T(512)S(1)}, f32[512]{0:T(512)S(1)}, u32[]{:S(2)}, u32[]{:S(2)}) collective-permute-start(f32[512]{0:T(512)S(1)} %select_add_fusion.1), channel_id=1, source_target_pairs={{9,0},{10,1},{11,2},{12,3},{13,4},{14,5},{15,6},{16,7},{17,8},{18,... | collective-permute-start | bytes 6152 | tf_op jit(solution)/shard_map/ppermute | solution.py:23
  53.0 11.1 %collective-permute-start.8 = (f32[512]{0:T(512)S(1)}, f32[512]{0:T(512)S(1)}, u32[]{:S(2)}, u32[]{:S(2)}) collective-permute-start(f32[512]{0:T(512)S(1)} %select_add_fusion.1), channel_id=1, source_target_pairs={{0,9},{1,10},{2,11},{3,12},{4,13},{5,14},{6,15},{7,16},{8,17},{9,1... | collective-permute-start | bytes 6152 | tf_op jit(solution)/shard_map/ppermute | solution.py:23
  58.2 6.0 collective-permute-start.9
  62.1 4.9 collective-permute-start.14
  67.1 6.5 copy-start
  76.2 11.5 %collective-permute-start.16 = (f32[512]{0:T(512)S(1)}, f32[512]{0:T(512)S(1)}, u32[]{:S(2)}, u32[]{:S(2)}) collective-permute-start(f32[512]{0:T(512)S(1)} %bitcast.368), channel_id=1, source_target_pairs={{9,0},{10,1},{11,2},{12,3},{13,4},{14,5},{15,6},{16,7},{17,8},{18,... | collective-permute-start | bytes 6152 | tf_op jit(solution)/shard_map/ppermute | solution.py:23
  77.5 19.2 %collective-permute-start.17 = (f32[512]{0:T(512)S(1)}, f32[512]{0:T(512)S(1)}, u32[]{:S(2)}, u32[]{:S(2)}) collective-permute-start(f32[512]{0:T(512)S(1)} %bitcast.365), channel_id=1, source_target_pairs={{8,0},{9,1},{10,2},{11,3},{12,4},{13,5},{14,6},{15,7},{16,8},{17,9... | collective-permute-start | bytes 6152 | tf_op jit(solution)/shard_map/ppermute | solution.py:23
  79.4 21.0 %collective-permute-start.18 = (f32[512]{0:T(512)S(1)}, f32[512]{0:T(512)S(1)}, u32[]{:S(2)}, u32[]{:S(2)}) collective-permute-start(f32[512]{0:T(512)S(1)} %bitcast.362), channel_id=1, source_target_pairs={{7,0},{8,1},{9,2},{10,3},{11,4},{12,5},{13,6},{14,7},{15,8},{16,9}... | collective-permute-start | bytes 6152 | tf_op jit(solution)/shard_map/ppermute | solution.py:23
  81.3 22.6 %collective-permute-start.19 = (f32[512]{0:T(512)S(1)}, f32[512]{0:T(512)S(1)}, u32[]{:S(2)}, u32[]{:S(2)}) collective-permute-start(f32[512]{0:T(512)S(1)} %bitcast.359), channel_id=1, source_target_pairs={{1,0},{2,1},{3,2},{4,3},{5,4},{6,5},{7,6},{8,7},{9,8},{10,9},{11,1... | collective-permute-start | bytes 6152 | tf_op jit(solution)/shard_map/ppermute | solution.py:23
  85.8 18.2 %collective-permute-start.20 = (f32[512]{0:T(512)S(1)}, f32[512]{0:T(512)S(1)}, u32[]{:S(2)}, u32[]{:S(2)}) collective-permute-start(f32[512]{0:T(512)S(1)} %bitcast.357), channel_id=1, source_target_pairs={{0,1},{1,2},{2,3},{3,4},{4,5},{5,6},{6,7},{7,8},{8,9},{9,10},{10,1... | collective-permute-start | bytes 6152 | tf_op jit(solution)/shard_map/ppermute | solution.py:23
  87.7 16.2 %collective-permute-start.21 = (f32[512]{0:T(512)S(1)}, f32[512]{0:T(512)S(1)}, u32[]{:S(2)}, u32[]{:S(2)}) collective-permute-start(f32[512]{0:T(512)S(1)} %bitcast.355), channel_id=1, source_target_pairs={{0,7},{1,8},{2,9},{3,10},{4,11},{5,12},{6,13},{7,14},{8,15},{9,16}... | collective-permute-start | bytes 6152 | tf_op jit(solution)/shard_map/ppermute | solution.py:23
  96.7 7.3 collective-permute-start.22
  100.4 3.6 collective-permute-start.23
  274.2 12.9 %collective-permute-start.26 = (f32[512]{0:T(512)S(1)}, f32[512]{0:T(512)S(1)}, u32[]{:S(2)}, u32[]{:S(2)}) collective-permute-start(f32[512]{0:T(512)S(1)} %multiply_add_fusion.12), channel_id=1, source_target_pairs={{0,7},{1,8},{2,9},{3,10},{4,11},{5,12},{6,13},{7,14},{8,15},{9,16}... | collective-permute-start | bytes 6152 | tf_op jit(solution)/shard_map/ppermute | solution.py:23
  276.9 15.6 %collective-permute-start.27 = (f32[512]{0:T(512)S(1)}, f32[512]{0:T(512)S(1)}, u32[]{:S(2)}, u32[]{:S(2)}) collective-permute-start(f32[512]{0:T(512)S(1)} %multiply_add_fusion.12), channel_id=1, source_target_pairs={{0,1},{1,2},{2,3},{3,4},{4,5},{5,6},{6,7},{7,8},{8,9},{9,10},{10,1... | collective-permute-start | bytes 6152 | tf_op jit(solution)/shard_map/ppermute | solution.py:23
  280.8 13.7 %collective-permute-start.28 = (f32[512]{0:T(512)S(1)}, f32[512]{0:T(512)S(1)}, u32[]{:S(2)}, u32[]{:S(2)}) collective-permute-start(f32[512]{0:T(512)S(1)} %multiply_add_fusion.12), channel_id=1, source_target_pairs={{1,0},{2,1},{3,2},{4,3},{5,4},{6,5},{7,6},{8,7},{9,8},{10,9},{11,1... | collective-permute-start | bytes 6152 | tf_op jit(solution)/shard_map/ppermute | solution.py:23
  283.7 14.3 %collective-permute-start.29 = (f32[512]{0:T(512)S(1)}, f32[512]{0:T(512)S(1)}, u32[]{:S(2)}, u32[]{:S(2)}) collective-permute-start(f32[512]{0:T(512)S(1)} %multiply_add_fusion.12), channel_id=1, source_target_pairs={{7,0},{8,1},{9,2},{10,3},{11,4},{12,5},{13,6},{14,7},{15,8},{16,9}... | collective-permute-start | bytes 6152 | tf_op jit(solution)/shard_map/ppermute | solution.py:23
  285.6 12.3 %collective-permute-start.31 = (f32[512]{0:T(512)S(1)}, f32[512]{0:T(512)S(1)}, u32[]{:S(2)}, u32[]{:S(2)}) collective-permute-start(f32[512]{0:T(512)S(1)} %multiply_add_fusion.12), channel_id=1, source_target_pairs={{9,0},{10,1},{11,2},{12,3},{13,4},{14,5},{15,6},{16,7},{17,8},{18,... | collective-permute-start | bytes 6152 | tf_op jit(solution)/shard_map/ppermute | solution.py:23
  287.1 10.9 %collective-permute-start.25 = (f32[512]{0:T(512)S(1)}, f32[512]{0:T(512)S(1)}, u32[]{:S(2)}, u32[]{:S(2)}) collective-permute-start(f32[512]{0:T(512)S(1)} %multiply_add_fusion.12), channel_id=1, source_target_pairs={{0,8},{1,9},{2,10},{3,11},{4,12},{5,13},{6,14},{7,15},{8,16},{9,17... | collective-permute-start | bytes 6152 | tf_op jit(solution)/shard_map/ppermute | solution.py:23
  292.5 5.5 collective-permute-start.30
  294.5 4.2 collective-permute-start.24
  305.0 149.2 %copy-start.2 = (f32[512,128]{1,0:T(8,128)S(1)}, f32[512,128]{1,0:T(8,128)}, u32[]{:S(2)}) copy-start(f32[512,128]{1,0:T(8,128)} %param.17) | copy-start | bytes 786436
  310.0 11.8 %collective-permute-start.32 = (f32[512]{0:T(512)S(1)}, f32[512]{0:T(512)S(1)}, u32[]{:S(2)}, u32[]{:S(2)}) collective-permute-start(f32[512]{0:T(512)S(1)} %bitcast.366), channel_id=1, source_target_pairs={{9,0},{10,1},{11,2},{12,3},{13,4},{14,5},{15,6},{16,7},{17,8},{18,... | collective-permute-start | bytes 6152 | tf_op jit(solution)/shard_map/ppermute | solution.py:23
  311.3 19.3 %collective-permute-start.33 = (f32[512]{0:T(512)S(1)}, f32[512]{0:T(512)S(1)}, u32[]{:S(2)}, u32[]{:S(2)}) collective-permute-start(f32[512]{0:T(512)S(1)} %bitcast.363), channel_id=1, source_target_pairs={{8,0},{9,1},{10,2},{11,3},{12,4},{13,5},{14,6},{15,7},{16,8},{17,9... | collective-permute-start | bytes 6152 | tf_op jit(solution)/shard_map/ppermute | solution.py:23
  313.2 21.6 %collective-permute-start.34 = (f32[512]{0:T(512)S(1)}, f32[512]{0:T(512)S(1)}, u32[]{:S(2)}, u32[]{:S(2)}) collective-permute-start(f32[512]{0:T(512)S(1)} %bitcast.360), channel_id=1, source_target_pairs={{7,0},{8,1},{9,2},{10,3},{11,4},{12,5},{13,6},{14,7},{15,8},{16,9}... | collective-permute-start | bytes 6152 | tf_op jit(solution)/shard_map/ppermute | solution.py:23
  315.2 23.1 %collective-permute-start.35 = (f32[512]{0:T(512)S(1)}, f32[512]{0:T(512)S(1)}, u32[]{:S(2)}, u32[]{:S(2)}) collective-permute-start(f32[512]{0:T(512)S(1)} %bitcast.358), channel_id=1, source_target_pairs={{1,0},{2,1},{3,2},{4,3},{5,4},{6,5},{7,6},{8,7},{9,8},{10,9},{11,1... | collective-permute-start | bytes 6152 | tf_op jit(solution)/shard_map/ppermute | solution.py:23
  319.9 18.4 %collective-permute-start.36 = (f32[512]{0:T(512)S(1)}, f32[512]{0:T(512)S(1)}, u32[]{:S(2)}, u32[]{:S(2)}) collective-permute-start(f32[512]{0:T(512)S(1)} %bitcast.356), channel_id=1, source_target_pairs={{0,1},{1,2},{2,3},{3,4},{4,5},{5,6},{6,7},{7,8},{8,9},{9,10},{10,1... | collective-permute-start | bytes 6152 | tf_op jit(solution)/shard_map/ppermute | solution.py:23
  321.8 16.5 %collective-permute-start.37 = (f32[512]{0:T(512)S(1)}, f32[512]{0:T(512)S(1)}, u32[]{:S(2)}, u32[]{:S(2)}) collective-permute-start(f32[512]{0:T(512)S(1)} %bitcast.354), channel_id=1, source_target_pairs={{0,7},{1,8},{2,9},{3,10},{4,11},{5,12},{6,13},{7,14},{8,15},{9,16}... | collective-permute-start | bytes 6152 | tf_op jit(solution)/shard_map/ppermute | solution.py:23
  330.7 7.7 %collective-permute-start.38 = (f32[512]{0:T(512)S(1)}, f32[512]{0:T(512)S(1)}, u32[]{:S(2)}, u32[]{:S(2)}) collective-permute-start(f32[512]{0:T(512)S(1)} %bitcast.352), channel_id=1, source_target_pairs={{0,8},{1,9},{2,10},{3,11},{4,12},{5,13},{6,14},{7,15},{8,16},{9,17... | collective-permute-start | bytes 6152 | tf_op jit(solution)/shard_map/ppermute | solution.py:23
  334.8 4.1 collective-permute-start.39
  427.2 62.1 %copy-start.4 = (f32[512]{0:T(512)}, f32[512]{0:T(512)S(1)}, u32[]{:S(2)}) copy-start(f32[512]{0:T(512)S(1)} %multiply_add_fusion.11) | copy-start | bytes 6148
  427.2 13.7 %collective-permute-start.42 = (f32[512]{0:T(512)S(1)}, f32[512]{0:T(512)S(1)}, u32[]{:S(2)}, u32[]{:S(2)}) collective-permute-start(f32[512]{0:T(512)S(1)} %multiply_add_fusion.11), channel_id=1, source_target_pairs={{0,7},{1,8},{2,9},{3,10},{4,11},{5,12},{6,13},{7,14},{8,15},{9,16}... | collective-permute-start | bytes 6152 | tf_op jit(solution)/shard_map/ppermute | solution.py:23
  430.9 14.7 %collective-permute-start.43 = (f32[512]{0:T(512)S(1)}, f32[512]{0:T(512)S(1)}, u32[]{:S(2)}, u32[]{:S(2)}) collective-permute-start(f32[512]{0:T(512)S(1)} %multiply_add_fusion.11), channel_id=1, source_target_pairs={{0,1},{1,2},{2,3},{3,4},{4,5},{5,6},{6,7},{7,8},{8,9},{9,10},{10,1... | collective-permute-start | bytes 6152 | tf_op jit(solution)/shard_map/ppermute | solution.py:23
  433.1 14.4 %collective-permute-start.44 = (f32[512]{0:T(512)S(1)}, f32[512]{0:T(512)S(1)}, u32[]{:S(2)}, u32[]{:S(2)}) collective-permute-start(f32[512]{0:T(512)S(1)} %multiply_add_fusion.11), channel_id=1, source_target_pairs={{1,0},{2,1},{3,2},{4,3},{5,4},{6,5},{7,6},{8,7},{9,8},{10,9},{11,1... | collective-permute-start | bytes 6152 | tf_op jit(solution)/shard_map/ppermute | solution.py:23
  437.7 14.1 %collective-permute-start.45 = (f32[512]{0:T(512)S(1)}, f32[512]{0:T(512)S(1)}, u32[]{:S(2)}, u32[]{:S(2)}) collective-permute-start(f32[512]{0:T(512)S(1)} %multiply_add_fusion.11), channel_id=1, source_target_pairs={{7,0},{8,1},{9,2},{10,3},{11,4},{12,5},{13,6},{14,7},{15,8},{16,9}... | collective-permute-start | bytes 6152 | tf_op jit(solution)/shard_map/ppermute | solution.py:23
  439.7 12.1 %collective-permute-start.47 = (f32[512]{0:T(512)S(1)}, f32[512]{0:T(512)S(1)}, u32[]{:S(2)}, u32[]{:S(2)}) collective-permute-start(f32[512]{0:T(512)S(1)} %multiply_add_fusion.11), channel_id=1, source_target_pairs={{9,0},{10,1},{11,2},{12,3},{13,4},{14,5},{15,6},{16,7},{17,8},{18,... | collective-permute-start | bytes 6152 | tf_op jit(solution)/shard_map/ppermute | solution.py:23
  441.0 10.9 %collective-permute-start.41 = (f32[512]{0:T(512)S(1)}, f32[512]{0:T(512)S(1)}, u32[]{:S(2)}, u32[]{:S(2)}) collective-permute-start(f32[512]{0:T(512)S(1)} %multiply_add_fusion.11), channel_id=1, source_target_pairs={{0,8},{1,9},{2,10},{3,11},{4,12},{5,13},{6,14},{7,15},{8,16},{9,17... | collective-permute-start | bytes 6152 | tf_op jit(solution)/shard_map/ppermute | solution.py:23
  445.6 6.2 collective-permute-start.46
  447.5 4.9 collective-permute-start.40
  455.8 33.1 %all-to-all-start = ((f32[3,512,128]{2,0,1:T(4,128)}), f32[3,512,128]{2,0,1:T(4,128)S(1)}, u32[]{:S(2)}, u32[]{:S(2)}) async-start(f32[3,512,128]{2,0,1:T(4,128)} %copy.161), calls=%async_computation | async-start | bytes 2097152 | tf_op jit(solution)/shard_map/all_to_all | solution.py:199
  491.3 3.8 copy-start.1
  607.7 5.9 copy-start.5
  607.7 8.0 %copy-start.6 = (f32[2]{0:T(128)S(1)}, f32[2]{0:T(128)}, u32[]{:S(2)}) copy-start(f32[2]{0:T(128)} %param.16) | copy-start | bytes 28
  607.7 12.8 %copy-start.7 = (f32[2]{0:T(128)S(1)}, f32[2]{0:T(128)}, u32[]{:S(2)}) copy-start(f32[2]{0:T(128)} %param.14) | copy-start | bytes 28
  609.9 44.0 %all-to-all-start.2 = ((f32[2,3,512,128]{2,0,1,3:T(2,128)}), f32[2,3,512,128]{2,0,1,3:T(2,128)S(1)}, u32[]{:S(2)}, u32[]{:S(2)}) async-start(f32[2,3,512,128]{2,0,1,3:T(2,128)} %copy.172), calls=%async_computation.2 | async-start | bytes 3145728 | tf_op jit(solution)/shard_map/all_to_all | solution.py:203
where the time goes:
time: 771 us; the launch traced here: 760 us
  blocking collectives  315 us (41%)
  starting transfers between devices  180 us (23%)
  local copies, waits for them, and re-layouts  123 us (16%)
  matrix products  61.8 us (8%)
  waiting for transfers between devices  55 us (7%)
  between operations  13.2 us (2%)
  other arithmetic  11.7 us (2%)
    psum x2, blocking collectives, squares(): return lax.psum(jnp.sum(residual * residual), ('row', 'col'))  166 us
    ppermute x48, starting transfers between devices, shifted(): return lax.ppermute(x, axis, pairs)  160 us
    psum x1, blocking collectives, on_device(): lax.psum(jnp.sum(direction * applied), ('row', 'col'))  86.3 us
    unnamed x22, local copies, waits for them, and re-layouts  52.5 us
    all_to_all x1, waiting for transfers between devices, on_device(): lax.all_to_all(lax.all_to_all(spectra, 'row', split_axis=3, concat_axis=2...  32.7 us
    all_to_all x1, blocking collectives, on_device(): lax.all_to_all(spectra, 'row', split_axis=3, concat_axis=2, tiled=True)  26.6 us
    all_to_all x1, blocking collectives, on_device(): lax.all_to_all(lax.all_to_all(stacked, 'row', split_axis=2, concat_axis=1...  20.9 us
    another operation x3, local copies, waits for them, and re-layouts, on_device(): spectra = jnp.stack([north_real, north_imag])  17.2 us
  transfers between devices with their start and end apart: 50, of which 7 were waited for; matrix products, arithmetic and copies ran while one was open for 0% of the time, Pallas kernels for 0%

commit v1 on v0

--- a/solution.py
+++ b/solution.py
@@ -229,7 +229,15 @@
     back_real, back_imag = transform_last(shaped_real, shaped_imag, 1.0)
     stacked = jnp.stack([back_real, back_imag]) / full_east
     returned = lax.all_to_all(
-        lax.all_to_all(stacked, "row", split_axis=2, concat_axis=1, tiled=True),
+        jnp.concatenate(
+            lax.all_to_all(
+                jnp.stack(jnp.split(stacked, lax.axis_size("row"), axis=2)),
+                concat_axis=0,
+                split_axis=0,
+                axis_name="row",
+            ),
+            axis=1,
+        ),
         "col",
         split_axis=2,
         concat_axis=1,

time: 771 us -> 745 us (0.966)
  local copies, waits for them, and re-layouts: 123 us -> 98.7 us
    unnamed x22 -> x51, local copies, waits for them, and re-layouts: 52.5 us -> 38.1 us
where the time goes in v1:
time: 745 us; the launch traced here: 734 us
  blocking collectives  315 us (42%)
  starting transfers between devices  181 us (24%)
  local copies, waits for them, and re-layouts  98.7 us (13%)
  matrix products  61.8 us (8%)
  waiting for transfers between devices  54.4 us (7%)
  between operations  13.8 us (2%)
  other arithmetic  9.91 us (1%)
    psum x2, blocking collectives, squares(): return lax.psum(jnp.sum(residual * residual), ('row', 'col'))  166 us
    ppermute x48, starting transfers between devices, shifted(): return lax.ppermute(x, axis, pairs)  160 us
    psum x1, blocking collectives, on_device(): lax.psum(jnp.sum(direction * applied), ('row', 'col'))  86.3 us
    unnamed x51, local copies, waits for them, and re-layouts  38.1 us
    all_to_all x1, waiting for transfers between devices, on_device(): lax.all_to_all(lax.all_to_all(spectra, 'row', split_axis=3, concat_axis=2...  32.1 us
    all_to_all x1, blocking collectives, on_device(): lax.all_to_all(spectra, 'row', split_axis=3, concat_axis=2, tiled=True)  26.6 us
    all_to_all x1, blocking collectives, on_device(): lax.all_to_all(jnp.concatenate(lax.all_to_all(jnp.stack(jnp.split(stacked...  20.6 us
    another operation x3, local copies, waits for them, and re-layouts, on_device(): spectra = jnp.stack([north_real, north_imag])  17.2 us
  transfers between devices with their start and end apart: 50, of which 7 were waited for; matrix products, arithmetic and copies ran while one was open for 0% of the time, Pallas kernels for 0%

profile of v1, /device:TPU:1, one launch (start us, length us, event | category | flops | bytes accessed | tf_op | source)
XLA Modules:
  0.0 734.1 jit_solution(11216628166609211613)
XLA Ops:
  1.3 4.7 fusion.8
  7.6 5.1 collective-permute-start.1
  14.7 5.0 collective-permute-start.3
  19.7 1.9 collective-permute-start.4
  21.6 7.7 %collective-permute-start.5 = (f32[512]{0:T(512)S(1)}, f32[512]{0:T(512)S(1)}, u32[]{:S(2)}, u32[]{:S(2)}) collective-permute-start(f32[512]{0:T(512)S(1)} %bitcast.469), channel_id=1, source_target_pairs={{0,7},{1,8},{2,9},{3,10},{4,11},{5,12},{6,13},{7,14},{8,15},{9,16}... | collective-permute-start | bytes 6152 | tf_op jit(solution)/shard_map/ppermute | solution.py:23
  29.4 5.0 collective-permute-start.6
  36.4 6.2 collective-permute-start.10
  42.6 5.2 collective-permute-start.11
  47.8 1.9 collective-permute-start.12
  49.7 1.9 collective-permute-start.13
  53.0 5.2 collective-permute-start.8
  58.2 3.9 collective-permute-start.9
  64.1 2.9 collective-permute-done.14
  67.3 6.2 fusion.6
  73.5 2.3 fusion.4
  79.4 1.9 collective-permute-start.18
  81.3 4.4 collective-permute-start.19
  87.7 9.0 %collective-permute-start.21 = (f32[512]{0:T(512)S(1)}, f32[512]{0:T(512)S(1)}, u32[]{:S(2)}, u32[]{:S(2)}) collective-permute-start(f32[512]{0:T(512)S(1)} %bitcast.477), channel_id=1, source_target_pairs={{0,7},{1,8},{2,9},{3,10},{4,11},{5,12},{6,13},{7,14},{8,15},{9,16}... | collective-permute-start | bytes 6152 | tf_op jit(solution)/shard_map/ppermute | solution.py:23
  96.7 3.7 collective-permute-start.22
  100.4 2.8 collective-permute-start.23
  104.7 91.9 %all-reduce = (f32[]{:T(128)}, f32[]{:T(128)}) all-reduce(f32[]{:T(128)} %get-tuple-element.3, f32[]{:T(128)} %get-tuple-element.2), channel_id=1, replica_groups=mesh['row'=32,'col'=8] {'row','col'}, use_global_device_ids=true, to_apply=%region_1.2 | all-reduce | flops 2 | bytes 16 | tf_op jit(solution)/shard_map/psum | solution.py:138
  198.5 74.3 %psum.30 = f32[]{:T(128)} all-reduce(f32[]{:T(128)} %multiply_reduce_fusion.1), channel_id=1, replica_groups=mesh['row'=32,'col'=8] {'row','col'}, use_global_device_ids=true, to_apply=%region_5.6 | all-reduce | flops 1 | bytes 8 | tf_op jit(solution)/shard_map/psum | solution.py:138
  274.2 2.7 collective-permute-start.26
  276.9 3.9 collective-permute-start.27
  280.8 2.9 collective-permute-start.28
  287.4 5.4 collective-permute-start.25
  294.7 3.5 collective-permute-start.24
  299.2 6.1 fusion.2
  305.3 4.7 fusion
  315.5 4.7 collective-permute-start.35
  322.1 8.8 %collective-permute-start.37 = (f32[512]{0:T(512)S(1)}, f32[512]{0:T(512)S(1)}, u32[]{:S(2)}, u32[]{:S(2)}) collective-permute-start(f32[512]{0:T(512)S(1)} %bitcast.476), channel_id=1, source_target_pairs={{0,7},{1,8},{2,9},{3,10},{4,11},{5,12},{6,13},{7,14},{8,15},{9,16}... | collective-permute-start | bytes 6152 | tf_op jit(solution)/shard_map/ppermute | solution.py:23
  330.9 4.2 collective-permute-start.38
  335.1 3.4 collective-permute-start.39
  339.9 86.3 %psum.31 = f32[]{:T(128)} all-reduce(f32[]{:T(128)} %multiply_reduce_fusion), channel_id=1, replica_groups=mesh['row'=32,'col'=8] {'row','col'}, use_global_device_ids=true, to_apply=%region_7.8 | all-reduce | flops 1 | bytes 8 | tf_op jit(solution)/shard_map/psum | solution.py:184
  427.5 3.7 collective-permute-start.42
  431.2 2.2 collective-permute-start.43
  433.4 4.6 collective-permute-start.44
  441.2 4.6 collective-permute-start.41
  447.8 4.2 collective-permute-start.40
  456.0 16.3 %all-to-all-start = ((f32[3,512,128]{2,0,1:T(4,128)}), f32[3,512,128]{2,0,1:T(4,128)S(1)}, u32[]{:S(2)}, u32[]{:S(2)}) async-start(f32[3,512,128]{2,0,1:T(4,128)} %copy.159), calls=%async_computation | async-start | bytes 2097152 | tf_op jit(solution)/shard_map/all_to_all | solution.py:199
  472.4 16.7 %all-to-all-done = f32[3,512,128]{2,0,1:T(4,128)S(1)} async-done(((f32[3,512,128]{2,0,1:T(4,128)}), f32[3,512,128]{2,0,1:T(4,128)S(1)}, u32[]{:S(2)}, u32[]{:S(2)}) %all-to-all-start) | async-done | bytes 786464 | tf_op jit(solution)/shard_map/all_to_all | solution.py:199
  492.9 2.4 fusion.26
  495.3 2.4 fusion.13
  497.7 2.0 copy.163
  499.7 2.3 stack_reshape.12
  502.0 3.7 fusion.12
  505.6 2.2 copy.166
  507.8 2.3 stack_reshape.13
  511.6 12.6 %copy.167 = f32[2,3,16,4096]{2,0,1,3:T(2,128)} copy(f32[2,3,16,4096]{3,2,1,0:T(8,128)S(1)} %pad_maximum_fusion) | data formatting | bytes 3145728 | tf_op jit(solution)/shard_map/stack | solution.py:202
  524.2 19.0 %reshape.247 = f32[32,1,12288]{2,1,0:T(1,128)S(1)} reshape(f32[4096,3,2,16]{3,2,1,0:T(2,128)} %bitcast.402) | data formatting | bytes 3145728
  543.2 26.6 %all_to_all.74 = f32[32,1,12288]{2,1,0:T(1,128)S(1)} all-to-all(f32[32,1,12288]{2,1,0:T(1,128)S(1)} %reshape.247), channel_id=1, replica_groups=mesh['row'=32,'col'=8] {'row'}, dimensions={0} | all-to-all | bytes 3145728 | tf_op jit(solution)/shard_map/all_to_all | solution.py:204
  570.3 4.4 reduce
  574.7 18.7 %reshape.248 = f32[4096,3,2,16]{3,2,1,0:T(2,128)} reshape(f32[32,12288]{1,0:T(8,128)S(1)} %reduce) | data formatting | bytes 3145728
  593.4 14.3 %copy.206 = f32[2,3,16,32,128]{4,2,3,1,0:T(8,128)S(1)} copy(f32[2,3,16,32,128]{2,0,1,4,3:T(2,128)} %bitcast.403) | data formatting | bytes 3145728 | tf_op jit(solution)/shard_map/all_to_all | solution.py:204
  607.8 2.2 copy.170
  609.9 4.0 all-to-all-start.2
  621.8 32.1 %all-to-all-done.2 = f32[2,3,512,128]{2,0,1,3:T(2,128)S(1)} async-done(((f32[2,3,512,128]{2,0,1,3:T(2,128)}), f32[2,3,512,128]{2,0,1,3:T(2,128)S(1)}, u32[]{:S(2)}, u32[]{:S(2)}) %all-to-all-start.2) | async-done | bytes 1572896 | tf_op jit(solution)/shard_map/all_to_all | solution.py:203
  678.4 15.2 %all_to_all.75 = f32[32,2,16,128]{3,2,1,0:T(8,128)S(1)} all-to-all(f32[32,2,16,128]{3,2,1,0:T(8,128)S(1)} %constant_dynamic-update-slice_fusion), channel_id=1, replica_groups=mesh['row'=32,'col'=8] {'row'}, dimensions={0} | all-to-all | bytes 1048576 | tf_op jit(solution)/shard_map/all_to_all | solution.py:233
  693.9 20.6 %all_to_all.76 = f32[2,512,128]{1,0,2:T(2,128)S(1)} all-to-all(f32[2,512,128]{1,0,2:T(2,128)S(1)} %copy.186), channel_id=1, replica_groups=mesh['row'=32,'col'=8] {'col'}, dimensions={2} | all-to-all | bytes 1048576 | tf_op jit(solution)/shard_map/all_to_all | solution.py:231
  714.7 2.8 reshape.228
  717.5 4.2 fusion.326
  721.7 2.2 copy.189
  723.9 1.9 fusion.138
  727.6 2.2 convolution_subtract_fusion.6
  (232 shorter events, 78.1 us)
Async XLA Ops:
  0.6 5.3 copy-start.3
  6.3 15.3 %collective-permute-start = (f32[512]{0:T(512)S(1)}, f32[512]{0:T(512)S(1)}, u32[]{:S(2)}, u32[]{:S(2)}) collective-permute-start(f32[512]{0:T(512)S(1)} %bitcast.489), channel_id=1, source_target_pairs={{9,0},{10,1},{11,2},{12,3},{13,4},{14,5},{15,6},{16,7},{17,8},{18,... | collective-permute-start | bytes 6152 | tf_op jit(solution)/shard_map/ppermute | solution.py:23
  7.6 21.8 %collective-permute-start.1 = (f32[512]{0:T(512)S(1)}, f32[512]{0:T(512)S(1)}, u32[]{:S(2)}, u32[]{:S(2)}) collective-permute-start(f32[512]{0:T(512)S(1)} %bitcast.486), channel_id=1, source_target_pairs={{8,0},{9,1},{10,2},{11,3},{12,4},{13,5},{14,6},{15,7},{16,8},{17,9... | collective-permute-start | bytes 6152 | tf_op jit(solution)/shard_map/ppermute | solution.py:23
  12.7 21.6 %collective-permute-start.2 = (f32[512]{0:T(512)S(1)}, f32[512]{0:T(512)S(1)}, u32[]{:S(2)}, u32[]{:S(2)}) collective-permute-start(f32[512]{0:T(512)S(1)} %bitcast.483), channel_id=1, source_target_pairs={{7,0},{8,1},{9,2},{10,3},{11,4},{12,5},{13,6},{14,7},{15,8},{16,9}... | collective-permute-start | bytes 6152 | tf_op jit(solution)/shard_map/ppermute | solution.py:23
  14.7 21.0 %collective-permute-start.3 = (f32[512]{0:T(512)S(1)}, f32[512]{0:T(512)S(1)}, u32[]{:S(2)}, u32[]{:S(2)}) collective-permute-start(f32[512]{0:T(512)S(1)} %bitcast.471), channel_id=1, source_target_pairs={{1,0},{2,1},{3,2},{4,3},{5,4},{6,5},{7,6},{8,7},{9,8},{10,9},{11,1... | collective-permute-start | bytes 6152 | tf_op jit(solution)/shard_map/ppermute | solution.py:23
  19.7 16.0 %collective-permute-start.4 = (f32[512]{0:T(512)S(1)}, f32[512]{0:T(512)S(1)}, u32[]{:S(2)}, u32[]{:S(2)}) collective-permute-start(f32[512]{0:T(512)S(1)} %bitcast.470), channel_id=1, source_target_pairs={{0,1},{1,2},{2,3},{3,4},{4,5},{5,6},{6,7},{7,8},{8,9},{9,10},{10,1... | collective-permute-start | bytes 6152 | tf_op jit(solution)/shard_map/ppermute | solution.py:23
  21.6 14.1 %collective-permute-start.5 = (f32[512]{0:T(512)S(1)}, f32[512]{0:T(512)S(1)}, u32[]{:S(2)}, u32[]{:S(2)}) collective-permute-start(f32[512]{0:T(512)S(1)} %bitcast.469), channel_id=1, source_target_pairs={{0,7},{1,8},{2,9},{3,10},{4,11},{5,12},{6,13},{7,14},{8,15},{9,16}... | collective-permute-start | bytes 6152 | tf_op jit(solution)/shard_map/ppermute | solution.py:23
  29.4 6.3 collective-permute-start.6
  34.3 2.0 collective-permute-start.7
  36.4 16.6 %collective-permute-start.10 = (f32[512]{0:T(512)S(1)}, f32[512]{0:T(512)S(1)}, u32[]{:S(2)}, u32[]{:S(2)}) collective-permute-start(f32[512]{0:T(512)S(1)} %select_add_fusion.1), channel_id=1, source_target_pairs={{0,7},{1,8},{2,9},{3,10},{4,11},{5,12},{6,13},{7,14},{8,15},{9,16}... | collective-permute-start | bytes 6152 | tf_op jit(solution)/shard_map/ppermute | solution.py:23
  42.6 15.6 %collective-permute-start.11 = (f32[512]{0:T(512)S(1)}, f32[512]{0:T(512)S(1)}, u32[]{:S(2)}, u32[]{:S(2)}) collective-permute-start(f32[512]{0:T(512)S(1)} %select_add_fusion.1), channel_id=1, source_target_pairs={{0,1},{1,2},{2,3},{3,4},{4,5},{5,6},{6,7},{7,8},{8,9},{9,10},{10,1... | collective-permute-start | bytes 6152 | tf_op jit(solution)/shard_map/ppermute | solution.py:23
  47.8 14.3 %collective-permute-start.12 = (f32[512]{0:T(512)S(1)}, f32[512]{0:T(512)S(1)}, u32[]{:S(2)}, u32[]{:S(2)}) collective-permute-start(f32[512]{0:T(512)S(1)} %select_add_fusion.1), channel_id=1, source_target_pairs={{1,0},{2,1},{3,2},{4,3},{5,4},{6,5},{7,6},{8,7},{9,8},{10,9},{11,1... | collective-permute-start | bytes 6152 | tf_op jit(solution)/shard_map/ppermute | solution.py:23
  49.7 14.3 %collective-permute-start.13 = (f32[512]{0:T(512)S(1)}, f32[512]{0:T(512)S(1)}, u32[]{:S(2)}, u32[]{:S(2)}) collective-permute-start(f32[512]{0:T(512)S(1)} %select_add_fusion.1), channel_id=1, source_target_pairs={{7,0},{8,1},{9,2},{10,3},{11,4},{12,5},{13,6},{14,7},{15,8},{16,9}... | collective-permute-start | bytes 6152 | tf_op jit(solution)/shard_map/ppermute | solution.py:23
  51.7 12.4 %collective-permute-start.15 = (f32[512]{0:T(512)S(1)}, f32[512]{0:T(512)S(1)}, u32[]{:S(2)}, u32[]{:S(2)}) collective-permute-start(f32[512]{0:T(512)S(1)} %select_add_fusion.1), channel_id=1, source_target_pairs={{9,0},{10,1},{11,2},{12,3},{13,4},{14,5},{15,6},{16,7},{17,8},{18,... | collective-permute-start | bytes 6152 | tf_op jit(solution)/shard_map/ppermute | solution.py:23
  53.0 11.1 %collective-permute-start.8 = (f32[512]{0:T(512)S(1)}, f32[512]{0:T(512)S(1)}, u32[]{:S(2)}, u32[]{:S(2)}) collective-permute-start(f32[512]{0:T(512)S(1)} %select_add_fusion.1), channel_id=1, source_target_pairs={{0,9},{1,10},{2,11},{3,12},{4,13},{5,14},{6,15},{7,16},{8,17},{9,1... | collective-permute-start | bytes 6152 | tf_op jit(solution)/shard_map/ppermute | solution.py:23
  58.2 6.0 collective-permute-start.9
  62.1 4.9 collective-permute-start.14
  67.1 6.5 copy-start
  76.2 11.5 %collective-permute-start.16 = (f32[512]{0:T(512)S(1)}, f32[512]{0:T(512)S(1)}, u32[]{:S(2)}, u32[]{:S(2)}) collective-permute-start(f32[512]{0:T(512)S(1)} %bitcast.490), channel_id=1, source_target_pairs={{9,0},{10,1},{11,2},{12,3},{13,4},{14,5},{15,6},{16,7},{17,8},{18,... | collective-permute-start | bytes 6152 | tf_op jit(solution)/shard_map/ppermute | solution.py:23
  77.5 19.2 %collective-permute-start.17 = (f32[512]{0:T(512)S(1)}, f32[512]{0:T(512)S(1)}, u32[]{:S(2)}, u32[]{:S(2)}) collective-permute-start(f32[512]{0:T(512)S(1)} %bitcast.487), channel_id=1, source_target_pairs={{8,0},{9,1},{10,2},{11,3},{12,4},{13,5},{14,6},{15,7},{16,8},{17,9... | collective-permute-start | bytes 6152 | tf_op jit(solution)/shard_map/ppermute | solution.py:23
  79.4 21.0 %collective-permute-start.18 = (f32[512]{0:T(512)S(1)}, f32[512]{0:T(512)S(1)}, u32[]{:S(2)}, u32[]{:S(2)}) collective-permute-start(f32[512]{0:T(512)S(1)} %bitcast.484), channel_id=1, source_target_pairs={{7,0},{8,1},{9,2},{10,3},{11,4},{12,5},{13,6},{14,7},{15,8},{16,9}... | collective-permute-start | bytes 6152 | tf_op jit(solution)/shard_map/ppermute | solution.py:23
  81.3 22.6 %collective-permute-start.19 = (f32[512]{0:T(512)S(1)}, f32[512]{0:T(512)S(1)}, u32[]{:S(2)}, u32[]{:S(2)}) collective-permute-start(f32[512]{0:T(512)S(1)} %bitcast.481), channel_id=1, source_target_pairs={{1,0},{2,1},{3,2},{4,3},{5,4},{6,5},{7,6},{8,7},{9,8},{10,9},{11,1... | collective-permute-start | bytes 6152 | tf_op jit(solution)/shard_map/ppermute | solution.py:23
  85.8 18.2 %collective-permute-start.20 = (f32[512]{0:T(512)S(1)}, f32[512]{0:T(512)S(1)}, u32[]{:S(2)}, u32[]{:S(2)}) collective-permute-start(f32[512]{0:T(512)S(1)} %bitcast.479), channel_id=1, source_target_pairs={{0,1},{1,2},{2,3},{3,4},{4,5},{5,6},{6,7},{7,8},{8,9},{9,10},{10,1... | collective-permute-start | bytes 6152 | tf_op jit(solution)/shard_map/ppermute | solution.py:23
  87.7 16.2 %collective-permute-start.21 = (f32[512]{0:T(512)S(1)}, f32[512]{0:T(512)S(1)}, u32[]{:S(2)}, u32[]{:S(2)}) collective-permute-start(f32[512]{0:T(512)S(1)} %bitcast.477), channel_id=1, source_target_pairs={{0,7},{1,8},{2,9},{3,10},{4,11},{5,12},{6,13},{7,14},{8,15},{9,16}... | collective-permute-start | bytes 6152 | tf_op jit(solution)/shard_map/ppermute | solution.py:23
  96.7 7.3 collective-permute-start.22
  100.4 3.6 collective-permute-start.23
  274.2 13.2 %collective-permute-start.26 = (f32[512]{0:T(512)S(1)}, f32[512]{0:T(512)S(1)}, u32[]{:S(2)}, u32[]{:S(2)}) collective-permute-start(f32[512]{0:T(512)S(1)} %multiply_add_fusion.12), channel_id=1, source_target_pairs={{0,7},{1,8},{2,9},{3,10},{4,11},{5,12},{6,13},{7,14},{8,15},{9,16}... | collective-permute-start | bytes 6152 | tf_op jit(solution)/shard_map/ppermute | solution.py:23
  276.9 15.9 %collective-permute-start.27 = (f32[512]{0:T(512)S(1)}, f32[512]{0:T(512)S(1)}, u32[]{:S(2)}, u32[]{:S(2)}) collective-permute-start(f32[512]{0:T(512)S(1)} %multiply_add_fusion.12), channel_id=1, source_target_pairs={{0,1},{1,2},{2,3},{3,4},{4,5},{5,6},{6,7},{7,8},{8,9},{9,10},{10,1... | collective-permute-start | bytes 6152 | tf_op jit(solution)/shard_map/ppermute | solution.py:23
  280.8 14.0 %collective-permute-start.28 = (f32[512]{0:T(512)S(1)}, f32[512]{0:T(512)S(1)}, u32[]{:S(2)}, u32[]{:S(2)}) collective-permute-start(f32[512]{0:T(512)S(1)} %multiply_add_fusion.12), channel_id=1, source_target_pairs={{1,0},{2,1},{3,2},{4,3},{5,4},{6,5},{7,6},{8,7},{9,8},{10,9},{11,1... | collective-permute-start | bytes 6152 | tf_op jit(solution)/shard_map/ppermute | solution.py:23
  283.7 14.5 %collective-permute-start.29 = (f32[512]{0:T(512)S(1)}, f32[512]{0:T(512)S(1)}, u32[]{:S(2)}, u32[]{:S(2)}) collective-permute-start(f32[512]{0:T(512)S(1)} %multiply_add_fusion.12), channel_id=1, source_target_pairs={{7,0},{8,1},{9,2},{10,3},{11,4},{12,5},{13,6},{14,7},{15,8},{16,9}... | collective-permute-start | bytes 6152 | tf_op jit(solution)/shard_map/ppermute | solution.py:23
  285.6 12.6 %collective-permute-start.31 = (f32[512]{0:T(512)S(1)}, f32[512]{0:T(512)S(1)}, u32[]{:S(2)}, u32[]{:S(2)}) collective-permute-start(f32[512]{0:T(512)S(1)} %multiply_add_fusion.12), channel_id=1, source_target_pairs={{9,0},{10,1},{11,2},{12,3},{13,4},{14,5},{15,6},{16,7},{17,8},{18,... | collective-permute-start | bytes 6152 | tf_op jit(solution)/shard_map/ppermute | solution.py:23
  287.4 10.9 %collective-permute-start.25 = (f32[512]{0:T(512)S(1)}, f32[512]{0:T(512)S(1)}, u32[]{:S(2)}, u32[]{:S(2)}) collective-permute-start(f32[512]{0:T(512)S(1)} %multiply_add_fusion.12), channel_id=1, source_target_pairs={{0,8},{1,9},{2,10},{3,11},{4,12},{5,13},{6,14},{7,15},{8,16},{9,17... | collective-permute-start | bytes 6152 | tf_op jit(solution)/shard_map/ppermute | solution.py:23
  292.8 5.5 collective-permute-start.30
  294.7 4.2 collective-permute-start.24
  305.3 149.1 %copy-start.2 = (f32[512,128]{1,0:T(8,128)S(1)}, f32[512,128]{1,0:T(8,128)}, u32[]{:S(2)}) copy-start(f32[512,128]{1,0:T(8,128)} %param.17) | copy-start | bytes 786436
  310.3 11.8 %collective-permute-start.32 = (f32[512]{0:T(512)S(1)}, f32[512]{0:T(512)S(1)}, u32[]{:S(2)}, u32[]{:S(2)}) collective-permute-start(f32[512]{0:T(512)S(1)} %bitcast.488), channel_id=1, source_target_pairs={{9,0},{10,1},{11,2},{12,3},{13,4},{14,5},{15,6},{16,7},{17,8},{18,... | collective-permute-start | bytes 6152 | tf_op jit(solution)/shard_map/ppermute | solution.py:23
  311.6 19.3 %collective-permute-start.33 = (f32[512]{0:T(512)S(1)}, f32[512]{0:T(512)S(1)}, u32[]{:S(2)}, u32[]{:S(2)}) collective-permute-start(f32[512]{0:T(512)S(1)} %bitcast.485), channel_id=1, source_target_pairs={{8,0},{9,1},{10,2},{11,3},{12,4},{13,5},{14,6},{15,7},{16,8},{17,9... | collective-permute-start | bytes 6152 | tf_op jit(solution)/shard_map/ppermute | solution.py:23
  313.5 21.6 %collective-permute-start.34 = (f32[512]{0:T(512)S(1)}, f32[512]{0:T(512)S(1)}, u32[]{:S(2)}, u32[]{:S(2)}) collective-permute-start(f32[512]{0:T(512)S(1)} %bitcast.482), channel_id=1, source_target_pairs={{7,0},{8,1},{9,2},{10,3},{11,4},{12,5},{13,6},{14,7},{15,8},{16,9}... | collective-permute-start | bytes 6152 | tf_op jit(solution)/shard_map/ppermute | solution.py:23
  315.5 23.1 %collective-permute-start.35 = (f32[512]{0:T(512)S(1)}, f32[512]{0:T(512)S(1)}, u32[]{:S(2)}, u32[]{:S(2)}) collective-permute-start(f32[512]{0:T(512)S(1)} %bitcast.480), channel_id=1, source_target_pairs={{1,0},{2,1},{3,2},{4,3},{5,4},{6,5},{7,6},{8,7},{9,8},{10,9},{11,1... | collective-permute-start | bytes 6152 | tf_op jit(solution)/shard_map/ppermute | solution.py:23
  320.2 18.4 %collective-permute-start.36 = (f32[512]{0:T(512)S(1)}, f32[512]{0:T(512)S(1)}, u32[]{:S(2)}, u32[]{:S(2)}) collective-permute-start(f32[512]{0:T(512)S(1)} %bitcast.478), channel_id=1, source_target_pairs={{0,1},{1,2},{2,3},{3,4},{4,5},{5,6},{6,7},{7,8},{8,9},{9,10},{10,1... | collective-permute-start | bytes 6152 | tf_op jit(solution)/shard_map/ppermute | solution.py:23
  322.1 16.5 %collective-permute-start.37 = (f32[512]{0:T(512)S(1)}, f32[512]{0:T(512)S(1)}, u32[]{:S(2)}, u32[]{:S(2)}) collective-permute-start(f32[512]{0:T(512)S(1)} %bitcast.476), channel_id=1, source_target_pairs={{0,7},{1,8},{2,9},{3,10},{4,11},{5,12},{6,13},{7,14},{8,15},{9,16}... | collective-permute-start | bytes 6152 | tf_op jit(solution)/shard_map/ppermute | solution.py:23
  330.9 7.7 %collective-permute-start.38 = (f32[512]{0:T(512)S(1)}, f32[512]{0:T(512)S(1)}, u32[]{:S(2)}, u32[]{:S(2)}) collective-permute-start(f32[512]{0:T(512)S(1)} %bitcast.474), channel_id=1, source_target_pairs={{0,8},{1,9},{2,10},{3,11},{4,12},{5,13},{6,14},{7,15},{8,16},{9,17... | collective-permute-start | bytes 6152 | tf_op jit(solution)/shard_map/ppermute | solution.py:23
  335.1 4.1 collective-permute-start.39
  427.5 62.1 %copy-start.4 = (f32[512]{0:T(512)}, f32[512]{0:T(512)S(1)}, u32[]{:S(2)}) copy-start(f32[512]{0:T(512)S(1)} %multiply_add_fusion.11) | copy-start | bytes 6148
  427.5 13.7 %collective-permute-start.42 = (f32[512]{0:T(512)S(1)}, f32[512]{0:T(512)S(1)}, u32[]{:S(2)}, u32[]{:S(2)}) collective-permute-start(f32[512]{0:T(512)S(1)} %multiply_add_fusion.11), channel_id=1, source_target_pairs={{0,7},{1,8},{2,9},{3,10},{4,11},{5,12},{6,13},{7,14},{8,15},{9,16}... | collective-permute-start | bytes 6152 | tf_op jit(solution)/shard_map/ppermute | solution.py:23
  431.2 14.7 %collective-permute-start.43 = (f32[512]{0:T(512)S(1)}, f32[512]{0:T(512)S(1)}, u32[]{:S(2)}, u32[]{:S(2)}) collective-permute-start(f32[512]{0:T(512)S(1)} %multiply_add_fusion.11), channel_id=1, source_target_pairs={{0,1},{1,2},{2,3},{3,4},{4,5},{5,6},{6,7},{7,8},{8,9},{9,10},{10,1... | collective-permute-start | bytes 6152 | tf_op jit(solution)/shard_map/ppermute | solution.py:23
  433.4 14.4 %collective-permute-start.44 = (f32[512]{0:T(512)S(1)}, f32[512]{0:T(512)S(1)}, u32[]{:S(2)}, u32[]{:S(2)}) collective-permute-start(f32[512]{0:T(512)S(1)} %multiply_add_fusion.11), channel_id=1, source_target_pairs={{1,0},{2,1},{3,2},{4,3},{5,4},{6,5},{7,6},{8,7},{9,8},{10,9},{11,1... | collective-permute-start | bytes 6152 | tf_op jit(solution)/shard_map/ppermute | solution.py:23
  438.0 14.1 %collective-permute-start.45 = (f32[512]{0:T(512)S(1)}, f32[512]{0:T(512)S(1)}, u32[]{:S(2)}, u32[]{:S(2)}) collective-permute-start(f32[512]{0:T(512)S(1)} %multiply_add_fusion.11), channel_id=1, source_target_pairs={{7,0},{8,1},{9,2},{10,3},{11,4},{12,5},{13,6},{14,7},{15,8},{16,9}... | collective-permute-start | bytes 6152 | tf_op jit(solution)/shard_map/ppermute | solution.py:23
  439.9 12.1 %collective-permute-start.47 = (f32[512]{0:T(512)S(1)}, f32[512]{0:T(512)S(1)}, u32[]{:S(2)}, u32[]{:S(2)}) collective-permute-start(f32[512]{0:T(512)S(1)} %multiply_add_fusion.11), channel_id=1, source_target_pairs={{9,0},{10,1},{11,2},{12,3},{13,4},{14,5},{15,6},{16,7},{17,8},{18,... | collective-permute-start | bytes 6152 | tf_op jit(solution)/shard_map/ppermute | solution.py:23
  441.2 10.9 %collective-permute-start.41 = (f32[512]{0:T(512)S(1)}, f32[512]{0:T(512)S(1)}, u32[]{:S(2)}, u32[]{:S(2)}) collective-permute-start(f32[512]{0:T(512)S(1)} %multiply_add_fusion.11), channel_id=1, source_target_pairs={{0,8},{1,9},{2,10},{3,11},{4,12},{5,13},{6,14},{7,15},{8,16},{9,17... | collective-permute-start | bytes 6152 | tf_op jit(solution)/shard_map/ppermute | solution.py:23
  445.9 6.2 collective-permute-start.46
  447.8 4.9 collective-permute-start.40
  456.0 33.1 %all-to-all-start = ((f32[3,512,128]{2,0,1:T(4,128)}), f32[3,512,128]{2,0,1:T(4,128)S(1)}, u32[]{:S(2)}, u32[]{:S(2)}) async-start(f32[3,512,128]{2,0,1:T(4,128)} %copy.159), calls=%async_computation | async-start | bytes 2097152 | tf_op jit(solution)/shard_map/all_to_all | solution.py:199
  491.5 3.8 copy-start.1
  607.7 6.2 copy-start.5
  607.7 8.2 %copy-start.6 = (f32[2]{0:T(128)S(1)}, f32[2]{0:T(128)}, u32[]{:S(2)}) copy-start(f32[2]{0:T(128)} %param.16) | copy-start | bytes 28
  607.8 13.3 %copy-start.7 = (f32[2]{0:T(128)S(1)}, f32[2]{0:T(128)}, u32[]{:S(2)}) copy-start(f32[2]{0:T(128)} %param.14) | copy-start | bytes 28
  609.9 44.0 %all-to-all-start.2 = ((f32[2,3,512,128]{2,0,1,3:T(2,128)}), f32[2,3,512,128]{2,0,1,3:T(2,128)S(1)}, u32[]{:S(2)}, u32[]{:S(2)}) async-start(f32[2,3,512,128]{2,0,1,3:T(2,128)} %copy.170), calls=%async_computation.2 | async-start | bytes 3145728 | tf_op jit(solution)/shard_map/all_to_all | solution.py:203
